TPU v7x, 32 devices: a whole 2x2x4 slice. The times are simulated.
32 devices in a mesh: band: 16 (over z, y, core), helper: 2 (over x).
Axes of the slice: x: 2, y: 2, z: 4, core: 2. Of those that a mesh axis runs over, the one named last changes fastest.
Arguments:
- node_latent: bfloat16 [2048, 256], P(('band', 'helper')), may hold values from -6 to 6
- edge_latent: bfloat16 [32768, 256], P(('band', 'helper')), may hold values from -6 to 6
- grad_out_node: bfloat16 [2048, 256], P(('band', 'helper')), may hold values from -6 to 6
- grad_out_edge: bfloat16 [32768, 256], P(('band', 'helper')), may hold values from -6 to 6
- senders: int32 [32768], P(('band', 'helper')), may hold values from 0 to 191
- receivers: int32 [32768], P(('band', 'helper')), may hold values from 0 to 127, as said below
- band_edges: int32 [16], replicated, may hold values from 2 to 16, as said below
- halo_list: int32 [16, 32], P('band'), may hold values from 0 to 127, as said below
- sea_mask: int32 [2048], P(('band', 'helper')), may hold values 0 or 1
- edge_w1: bfloat16 [768, 256], replicated, may hold values from -0.21875 to 0.21875
- edge_b1: float32 [256], replicated, may hold values from -3 to 3
- edge_w2: bfloat16 [256, 256], replicated, may hold values from -0.375 to 0.375
- edge_b2: float32 [256], replicated, may hold values from -3 to 3
- node_w1: bfloat16 [512, 256], replicated, may hold values from -0.25 to 0.25
- node_b1: float32 [256], replicated, may hold values from -3 to 3
- node_w2: bfloat16 [256, 256], replicated, may hold values from -0.375 to 0.375
- node_b2: float32 [256], replicated, may hold values from -3 to 3
Outputs:
- grad_node: float32 [2048, 256], P(('band', 'helper'))
- grad_edge: bfloat16 [32768, 256], P(('band', 'helper'))
- grad_edge_w1: float32 [768, 256], replicated
- grad_edge_b1: float32 [256], replicated
- grad_edge_w2: float32 [256, 256], replicated
- grad_edge_b2: float32 [256], replicated
- grad_node_w1: float32 [512, 256], replicated
- grad_node_b1: float32 [256], replicated
- grad_node_w2: float32 [256, 256], replicated
- grad_node_b2: float32 [256], replicated
Inputs may be any that keep to these rules, and one draw needn't show every extreme that they name: In every aligned block of 128 edge rows, all receivers lie in one aligned tile of 64 nodes. `band_edges`: A quarter of the bands, consecutive along the cycle, hold 16 live blocks; every other band holds between 2 and 6. `halo_list`: the 32 entries of a band are distinct.
All inputs are finite; a program needn't handle non-finite values. No bound on the sum of `sea_mask` on one device may be relied on, other than what follows from the above.
Results may differ from a plain program's by a relative error of at most 0.01.
Values may be sent and summed in bfloat16 or wider, within the bound.
No kernel may reach another device: no remote copies, remote signals or barrier semaphores. Data moves between devices by JAX's collectives and lax.ppermute only.
A program may use at most 64 MiB of HBM per device.

v0:
```python
import math
import jax
import jax.numpy as jnp
from jax import lax
from jax.sharding import PartitionSpec as P

EB = 128
RTILE = 64
norm_eps = 1e-05


def passed_along(array, axis, by):
    count = lax.axis_size(axis)
    return lax.ppermute(array, axis, [(i, (i + by) % count) for i in range(count)])


def layer_norm(pre_act):
    row_mean = jnp.mean(pre_act, axis=-1, keepdims=True)
    centre = pre_act - row_mean
    inv_dev = lax.rsqrt(jnp.mean(centre * centre, axis=-1, keepdims=True) + norm_eps)
    return (centre * inv_dev, inv_dev)


def norm_back(grad_in, normed, inv_dev):
    return inv_dev * (
        grad_in
        - jnp.mean(grad_in, axis=-1, keepdims=True)
        - normed * jnp.mean(grad_in * normed, axis=-1, keepdims=True)
    )


def silu_slope(pre_act):
    sigmoid_v = jax.nn.sigmoid(pre_act)
    return sigmoid_v * (1.0 + pre_act * (1.0 - sigmoid_v))


def dot_left_t(left_op, right_op):
    return lax.dot_general(
        left_op, right_op, (((0,), (0,)), ((), ())), preferred_element_type=jnp.float32
    )


def dot_right_t(left_op, right_op):
    return lax.dot_general(
        left_op, right_op, (((1,), (1,)), ((), ())), preferred_element_type=jnp.float32
    )


def mlp_forward(inputs, w_first, b_first, w_second, b_second):
    pre_act = jnp.dot(inputs, w_first, preferred_element_type=jnp.float32) + b_first
    hidden = jax.nn.silu(pre_act).astype(jnp.bfloat16)
    normed, inv_dev = layer_norm(
        jnp.dot(hidden, w_second, preferred_element_type=jnp.float32) + b_second
    )
    return (pre_act, hidden, normed, inv_dev)


def mlp_back_parts(inputs, w_second, pre_act, hidden, normed, inv_dev, grad_out):
    grad_second = norm_back(grad_out, normed, inv_dev)
    second_b = grad_second.astype(jnp.bfloat16)
    gw_second = dot_left_t(hidden, second_b)
    gb_second = jnp.sum(grad_second, axis=0)
    grad_first = dot_right_t(second_b, w_second) * silu_slope(pre_act)
    first_b = grad_first.astype(jnp.bfloat16)
    gw_first = dot_left_t(inputs, first_b)
    gb_first = jnp.sum(grad_first, axis=0)
    return (first_b, gw_first, gb_first, gw_second, gb_second)


def mlp_backward(inputs, w_first, w_second, pre_act, hidden, normed, inv_dev, grad_out):
    parts = mlp_back_parts(inputs, w_second, pre_act, hidden, normed, inv_dev, grad_out)
    return (dot_right_t(parts[0], w_first),) + parts[1:]


def tile_sum(running, recv_ids, values):
    tile_base = recv_ids[0] // RTILE * RTILE
    local_ids = recv_ids - tile_base
    onehot = local_ids[:, None] == jnp.arange(RTILE, dtype=jnp.int32)[None, :]
    if values.dtype == jnp.bfloat16:
        tile_part = dot_left_t(onehot.astype(jnp.bfloat16), values)
    else:
        tile_part = lax.dot_general(
            onehot.astype(jnp.float32),
            values,
            (((0,), (0,)), ((), ())),
            precision=lax.Precision.HIGHEST,
            preferred_element_type=jnp.float32,
        )
    current = lax.dynamic_slice_in_dim(running, tile_base, RTILE, 0)
    return lax.dynamic_update_slice_in_dim(running, current + tile_part, tile_base, 0)


def on_device(
    node_latent,
    edge_latent,
    grad_out_node,
    grad_out_edge,
    senders,
    receivers,
    band_edges,
    halo_list,
    sea_mask,
    edge_w1,
    edge_b1,
    edge_w2,
    edge_b2,
    node_w1,
    node_b1,
    node_w2,
    node_b2,
):
    features = node_latent.shape[1]
    helpers = lax.axis_size("helper")
    band_count = lax.axis_size("band")
    helper_idx = lax.axis_index("helper")
    band_idx = lax.axis_index("band")
    node_dev = node_latent.shape[0]
    band_size = node_dev * helpers
    halo_size = halo_list.shape[1]
    edge_block = EB
    slot_count = edge_latent.shape[0] // edge_block
    edge_blocks = edge_latent.reshape(slot_count, edge_block, features)
    grad_blocks = grad_out_edge.reshape(slot_count, edge_block, features)
    send_blocks = senders.reshape(slot_count, edge_block)
    recv_blocks = receivers.reshape(slot_count, edge_block)
    halo_ids = halo_list[0]
    band_rows = lax.all_gather(node_latent, "helper", axis=0, tiled=True)
    outgoing = band_rows[halo_ids]
    from_prev = passed_along(outgoing, "band", 1)
    from_next = passed_along(outgoing, "band", -1)
    lookup = jnp.concatenate([band_rows, from_prev, from_next], axis=0)
    live_count = band_edges[band_idx]
    own_live = jnp.clip((live_count - helper_idx + helpers - 1) // helpers, 0, slot_count)

    def inputs_of(slot_id):
        return jnp.concatenate(
            [lookup[send_blocks[slot_id]], band_rows[recv_blocks[slot_id]], edge_blocks[slot_id]],
            axis=1,
        )

    def message_of(inputs):
        normed = mlp_forward(inputs, edge_w1, edge_b1, edge_w2, edge_b2)[2]
        return normed.astype(jnp.bfloat16)

    def add_own(slot_id, agg_rows):
        return tile_sum(agg_rows, recv_blocks[slot_id], message_of(inputs_of(slot_id)))

    agg_start = jnp.zeros((band_size, features), jnp.float32)
    agg_rows = lax.fori_loop(0, own_live, add_own, agg_start)
    agg_own = lax.psum_scatter(agg_rows, "helper", scatter_dimension=0, tiled=True)
    node_in = jnp.concatenate([node_latent, agg_own.astype(jnp.bfloat16)], axis=1)
    n_pre, n_hidden, n_normed, n_inv = mlp_forward(node_in, node_w1, node_b1, node_w2, node_b2)
    node_seed = sea_mask[:, None].astype(jnp.float32) * grad_out_node.astype(jnp.float32)
    node_back = mlp_backward(node_in, node_w1, node_w2, n_pre, n_hidden, n_normed, n_inv, node_seed)
    agg_grad = node_back[0][:, features:].astype(jnp.bfloat16)
    agg_band = lax.all_gather(agg_grad, "helper", axis=0, tiled=True)

    def edge_parts(inputs, grad_edge_in, agg_rows_in):
        msg_grad = grad_edge_in.astype(jnp.float32) + agg_rows_in.astype(jnp.float32)
        pre_act, hidden, normed, inv_dev = mlp_forward(inputs, edge_w1, edge_b1, edge_w2, edge_b2)
        return mlp_back_parts(inputs, edge_w2, pre_act, hidden, normed, inv_dev, msg_grad)

    def settle(lookup_grad, edge_out, slot_id, first_b):
        grad_inputs = dot_right_t(first_b, edge_w1)
        lookup_grad = lookup_grad.at[send_blocks[slot_id]].add(grad_inputs[:, :features])
        lookup_grad = tile_sum(
            lookup_grad, recv_blocks[slot_id], grad_inputs[:, features : 2 * features]
        )
        edge_new = (
            grad_blocks[slot_id].astype(jnp.float32) + grad_inputs[:, 2 * features :]
        ).astype(jnp.bfloat16)
        return (lookup_grad, edge_out.at[slot_id].set(edge_new))

    def own_step(slot_id, loop_state):
        first_b, gw_one, gb_one, gw_two, gb_two = edge_parts(
            inputs_of(slot_id), grad_blocks[slot_id], agg_band[recv_blocks[slot_id]]
        )
        lookup_grad, edge_out = settle(loop_state[0], loop_state[1], slot_id, first_b)
        return (
            lookup_grad,
            edge_out,
            loop_state[2] + gw_one,
            loop_state[3] + gb_one,
            loop_state[4] + gw_two,
            loop_state[5] + gb_two,
        )

    start_state = (
        jnp.zeros((band_size + 2 * halo_size, features), jnp.float32),
        jnp.zeros((slot_count, edge_block, features), jnp.bfloat16),
        jnp.zeros(edge_w1.shape, jnp.float32),
        jnp.zeros((features,), jnp.float32),
        jnp.zeros(edge_w2.shape, jnp.float32),
        jnp.zeros((features,), jnp.float32),
    )
    final_state = lax.fori_loop(0, own_live, own_step, start_state)
    lookup_grad, edge_out = (final_state[0], final_state[1])
    edge_wgrads = final_state[2:]
    band_grad = lookup_grad[:band_size]
    prev_region = lookup_grad[band_size : band_size + halo_size]
    next_region = lookup_grad[band_size + halo_size :]
    from_next_band = passed_along(prev_region.astype(jnp.bfloat16), "band", -1).astype(
        prev_region.dtype
    )
    from_prev_band = passed_along(next_region.astype(jnp.bfloat16), "band", 1).astype(
        next_region.dtype
    )
    band_grad = band_grad.at[halo_ids].add(from_next_band + from_prev_band)
    node_sum = lax.psum_scatter(
        band_grad.astype(jnp.bfloat16), "helper", scatter_dimension=0, tiled=True
    ).astype(jnp.float32)
    grad_node = node_sum + grad_out_node.astype(jnp.float32) + node_back[0][:, :features]
    edge_scale = 1.0 / math.sqrt(slot_count * edge_block * helpers * band_count)
    node_scale = 1.0 / math.sqrt(node_dev * helpers * band_count)
    sums = lax.psum(
        (
            edge_wgrads[0] * edge_scale,
            edge_wgrads[1] * edge_scale,
            edge_wgrads[2] * edge_scale,
            edge_wgrads[3] * edge_scale,
            node_back[1] * node_scale,
            node_back[2] * node_scale,
            node_back[3] * node_scale,
            node_back[4] * node_scale,
        ),
        ("band", "helper"),
    )
    grad_edge = edge_out.reshape(slot_count * edge_block, features)
    return (
        grad_node,
        grad_edge,
        sums[0],
        sums[1],
        sums[2],
        sums[3],
        sums[4],
        sums[5],
        sums[6],
        sums[7],
    )


def solution(mesh):
    in_specs = (
        P(("band", "helper"), None),
        P(("band", "helper"), None),
        P(("band", "helper"), None),
        P(("band", "helper"), None),
        P(("band", "helper")),
        P(("band", "helper")),
        P(),
        P("band", None),
        P(("band", "helper")),
        P(),
        P(),
        P(),
        P(),
        P(),
        P(),
        P(),
        P(),
    )
    out_specs = (
        P(("band", "helper"), None),
        P(("band", "helper"), None),
        P(),
        P(),
        P(),
        P(),
        P(),
        P(),
        P(),
        P(),
    )
    return jax.shard_map(
        on_device, mesh=mesh, in_specs=in_specs, out_specs=out_specs, check_vma=False
    )
```

profile of v0, /device:TPU:0, one launch (start us, length us, event | category | flops | bytes accessed | tf_op | source)
XLA Modules:
  0.0 384.1 jit_solution(12179185624823476819)
XLA Ops:
  7.3 5.9 %all_gather.6 = bf16[128,256]{1,0:T(8,128)(2,1)S(1)} all-gather(bf16[64,256]{1,0:T(8,128)(2,1)} %param.23), channel_id=1, replica_groups=mesh['band'=16,'helper'=2] {'helper'}, dimensions={0}, use_global_device_ids=true | all-gather | bytes 98304 | tf_op jit(solution)/shard_map/all_gather | solution.py:127
  14.5 4.4 %collective-permute-start.1 = (bf16[32,256]{1,0:T(8,128)(2,1)S(1)}, bf16[32,256]{1,0:T(8,128)(2,1)S(1)}, u32[]{:S(2)}, u32[]{:S(2)}) collective-permute-start(bf16[32,256]{1,0:T(8,128)(2,1)S(1)} %gather_fusion.5), channel_id=1, source_target_pairs={{0,30},{2,0},{4,2},{6,4},{8,6},{10,8},{12,10},{14,12},{16,14},{18,... | collective-permute-start | bytes 49160 | tf_op jit(solution)/shard_map/ppermute | solution.py:14
  21.5 11.5 %while.35 = (s32[]{:T(128)}, f32[128,256]{1,0:T(8,128)S(1)}, s32[]{:T(128)}, s32[8,128]{1,0:T(8,128)}, s32[8,128]{1,0:T(8,128)}, /*index=5*/bf16[192,256]{1,0:T(...) while((s32[]{:T(128)}, f32[128,256]{1,0:T(8,128)S(1)}, ...), condition=%wide.region_3.4_spmd, body=%wide.region_0.3_spmd.sunk | while | flops 72379416 | bytes 1659831 | solution.py:149
  22.4 0.9 dynamic-slice_bitcast_fusion.4
  23.3 0.8 gather_fusion
  24.8 0.8 gather_fusion.1
  25.7 1.1 fusion.120
  28.2 0.9 dynamic-slice_bitcast_fusion.4
  29.0 0.8 gather_fusion
  30.6 0.8 gather_fusion.1
  31.5 1.1 fusion.120
  34.4 42.2 %reduce-scatter.3.cloned.1.call-done = f32[64,256]{1,0:T(8,128)} async-done(((f32[128,256]{1,0:T(8,128)}), f32[64,256]{1,0:T(8,128)}) %reduce-scatter.3.cloned.1.call-update) | async-done | bytes 65552 | tf_op jit(solution)/shard_map/reduce_scatter | solution.py:150
  76.6 0.8 convert_element_type.89
  80.3 0.8 fusion.70
  81.3 1.0 convolution_multiply_fusion.1
  82.4 4.6 %all_gather.7 = bf16[128,256]{1,0:T(8,128)(2,1)S(1)} all-gather(bf16[64,256]{1,0:T(8,128)(2,1)S(1)} %slice.106), channel_id=1, replica_groups=mesh['band'=16,'helper'=2] {'helper'}, dimensions={0}, use_global_device_ids=true | all-gather | bytes 98304 | tf_op jit(solution)/shard_map/all_gather | solution.py:156
  87.1 32.5 %while.36 = (s32[]{:T(128)}, f32[192,256]{1,0:T(8,128)S(1)}, bf16[8,128,256]{2,1,0:T(8,128)(2,1)S(1)}, f32[768,256]{1,0:T(8,128)S(1)}, f32[256]{0:T(256)S(1)}, /...) while((s32[]{:T(128)}, f32[192,256]{1,0:T(8,128)S(1)}, ...), condition=%wide.region_18.19_spmd, body=%wide.region_9.18_spmd.sunk | while | flops 229600272 | bytes 8176405 | solution.py:196
  87.9 0.8 dynamic-slice_bitcast_fusion.5
  89.4 0.8 gather_fusion.2
  90.3 0.8 gather_fusion.3
  91.4 0.8 gather_fusion.4
  92.3 0.9 fusion.134
  93.4 1.0 fusion.135
  94.5 1.0 fusion.136
  95.5 0.8 fusion.137
  96.5 1.5 scatter_custom_fusion.7
  99.9 1.5 fusion.140
  104.1 0.8 dynamic-slice_bitcast_fusion.5
  105.6 0.8 gather_fusion.2
  106.5 0.8 gather_fusion.3
  107.6 0.8 gather_fusion.4
  108.4 0.9 fusion.134
  109.6 1.0 fusion.135
  110.6 1.0 fusion.136
  111.7 0.8 fusion.137
  112.7 1.5 scatter_custom_fusion.7
  116.1 1.5 fusion.140
  119.6 14.7 %collective-permute-start.3 = (bf16[32,256]{1,0:T(8,128)(2,1)S(1)}, bf16[32,256]{1,0:T(8,128)(2,1)S(1)}, u32[]{:S(2)}, u32[]{:S(2)}) collective-permute-start(bf16[32,256]{1,0:T(8,128)(2,1)S(1)} %get-tuple-element.515), channel_id=1, source_target_pairs={{0,2},{2,4},{4,6},{6,8},{8,10},{10,12},{12,14},{14,16},{16,18},{18... | collective-permute-start | bytes 49160 | tf_op jit(solution)/shard_map/ppermute | solution.py:14
  134.3 3.9 %collective-permute-start.2 = (bf16[32,256]{1,0:T(8,128)(2,1)S(1)}, bf16[32,256]{1,0:T(8,128)(2,1)S(1)}, u32[]{:S(2)}, u32[]{:S(2)}) collective-permute-start(bf16[32,256]{1,0:T(8,128)(2,1)S(1)} %get-tuple-element.514), channel_id=1, source_target_pairs={{0,30},{2,0},{4,2},{6,4},{8,6},{10,8},{12,10},{14,12},{16,14},{18,... | collective-permute-start | bytes 49160 | tf_op jit(solution)/shard_map/ppermute | solution.py:14
  138.2 1.0 broadcast_multiply_fusion.4
  139.9 79.1 %collective-permute-done.2 = bf16[32,256]{1,0:T(8,128)(2,1)S(1)} collective-permute-done((bf16[32,256]{1,0:T(8,128)(2,1)S(1)}, bf16[32,256]{1,0:T(8,128)(2,1)S(1)}, u32[]{:S(2)}, u32[]{:S(2)}) %collective-permute-start.2) | collective-permute-done | bytes 16416 | tf_op jit(solution)/shard_map/ppermute | solution.py:14
  219.0 1.0 scatter_custom_fusion.1
  221.5 0.9 convolution_multiply_fusion.2
  223.9 41.4 %all-reduce = (f32[256]{0:T(256)}, f32[256]{0:T(256)}, f32[256]{0:T(256)}, f32[256]{0:T(256)}) all-reduce(f32[256]{0:T(256)S(1)} %broadcast_multiply_fusion.9, f32[256]{0:T(256)S(1)} %broadcast_multiply_fusion.8, f32[256]{0:T(256)S(1)} %broadcast_multiply_fusion.7, ...), channel_id=1, replica_groups=mesh['band'=16,'helper'=2] {'band','helper'}, use_global_device_ids=true, to_apply=%region_22.23 | all-reduce | flops 1024 | bytes 8192 | tf_op jit(solution)/shard_map/psum | solution.py:215
  265.3 1.4 fusion.47
  266.7 105.9 %all-reduce.4.cloned.1.call-done = (f32[768,256]{1,0:T(8,128)}, f32[256,256]{1,0:T(8,128)}, f32[512,256]{1,0:T(8,128)}, f32[256,256]{1,0:T(8,128)}) async-done(((f32[768,256]{1,0:T(8,128)}, f32[256,256]{1,0:T(8,128)}, f32[512,256]{1,0:T(8,128)}, f32[256,256]{1,0:T(8,128)}), (f32[768,256]{1,0:T(8,128)}, f32[256,256]{1,0:T(8,128)}, f32[512,256]{1,0:T(8,128)}, ...) | async-done | bytes 1835024 | tf_op jit(solution)/shard_map/psum | solution.py:215
  372.6 2.1 copy.65
  375.8 0.8 copy.67
  (179 shorter events, 28.7 us)
Async XLA Ops:
  7.2 70.3 %copy-start = (bf16[512,256]{1,0:T(8,128)(2,1)S(1)}, bf16[512,256]{1,0:T(8,128)(2,1)}, u32[]{:S(2)}) copy-start(bf16[512,256]{1,0:T(8,128)(2,1)} %param.36) | copy-start | bytes 786436
  7.2 6.0 %copy-start.30 = (s32[1,32]{1,0:T(1,128)S(1)}, s32[1,32]{1,0:T(1,128)}, u32[]{:S(2)}) copy-start(s32[1,32]{1,0:T(1,128)} %param.30) | copy-start | bytes 388
  7.2 13.7 %copy-start.1 = (bf16[768,256]{1,0:T(8,128)(2,1)S(1)}, bf16[768,256]{1,0:T(8,128)(2,1)}, u32[]{:S(2)}) copy-start(bf16[768,256]{1,0:T(8,128)(2,1)} %param.32) | copy-start | bytes 1179652
  7.2 69.4 %reduce-scatter.3.cloned.1.call-start = ((), (), s32[]{:S(2)}) async-start(), calls=%async_computation.2 | async-start | bytes 196608 | tf_op jit(solution)/shard_map/reduce_scatter | solution.py:150
  13.2 0.6 copy-start.21
  14.4 6.4 %collective-permute-start = (bf16[32,256]{1,0:T(8,128)(2,1)S(1)}, bf16[32,256]{1,0:T(8,128)(2,1)S(1)}, u32[]{:S(2)}, u32[]{:S(2)}) collective-permute-start(bf16[32,256]{1,0:T(8,128)(2,1)S(1)} %gather_fusion.5), channel_id=1, source_target_pairs={{0,2},{2,4},{4,6},{6,8},{8,10},{10,12},{12,14},{14,16},{16,18},{18... | collective-permute-start | bytes 49160 | tf_op jit(solution)/shard_map/ppermute | solution.py:14
  14.5 6.4 %collective-permute-start.1 = (bf16[32,256]{1,0:T(8,128)(2,1)S(1)}, bf16[32,256]{1,0:T(8,128)(2,1)S(1)}, u32[]{:S(2)}, u32[]{:S(2)}) collective-permute-start(bf16[32,256]{1,0:T(8,128)(2,1)S(1)} %gather_fusion.5), channel_id=1, source_target_pairs={{0,30},{2,0},{4,2},{6,4},{8,6},{10,8},{12,10},{14,12},{16,14},{18,... | collective-permute-start | bytes 49160 | tf_op jit(solution)/shard_map/ppermute | solution.py:14
  18.9 0.7 copy-start.31
  18.9 2.0 copy-start.23
  20.9 0.7 copy-start.27
  33.1 0.7 copy-start.2
  33.8 0.7 copy-start.32
  33.8 231.5 %reduce-scatter.5.cloned.1.call-start = ((), (), s32[]{:S(2)}) async-start(), calls=%async_computation.3 | async-start | bytes 98304 | tf_op jit(solution)/shard_map/reduce_scatter | solution.py:209
  34.4 43.0 %copy-start.7 = (bf16[64,256]{1,0:T(8,128)(2,1)S(1)}, bf16[64,256]{1,0:T(8,128)(2,1)}, u32[]{:S(2)}) copy-start(bf16[64,256]{1,0:T(8,128)(2,1)} %param.23) | copy-start | bytes 98308
  34.4 43.0 %copy-start.19 = (f32[256]{0:T(256)S(1)}, f32[256]{0:T(256)}, u32[]{:S(2)}) copy-start(f32[256]{0:T(256)} %param.37) | copy-start | bytes 3076
  77.5 0.9 copy-start.22
  77.5 0.9 copy-start.26
  78.4 1.9 copy-start.11
  78.6 0.8 copy-start.8
  80.3 0.8 copy-start.13
  81.3 1.1 copy-start.5
  87.1 4.0 %copy-start.28 = (f32[256]{0:T(256)}, f32[256]{0:T(256)S(1)}, u32[]{:S(2)}) copy-start(f32[256]{0:T(256)S(1)} %get-tuple-element.884) | copy-start | bytes 3076 | tf_op jit(solution)/shard_map/while
  87.1 8.3 %copy-start.24 = (bf16[256,256]{1,0:T(8,128)(2,1)}, bf16[256,256]{1,0:T(8,128)(2,1)S(1)}, u32[]{:S(2)}) copy-start(bf16[256,256]{1,0:T(8,128)(2,1)S(1)} %get-tuple-element.885) | copy-start | bytes 393220 | tf_op jit(solution)/shard_map/while
  87.9 2.4 copy-start.16
  98.5 0.7 copy-start.17
  101.7 0.7 copy-start.15
  102.4 0.9 copy-start.25
  102.7 0.7 copy-start.29
  103.4 4.0 %copy-start.28 = (f32[256]{0:T(256)}, f32[256]{0:T(256)S(1)}, u32[]{:S(2)}) copy-start(f32[256]{0:T(256)S(1)} %get-tuple-element.884) | copy-start | bytes 3076 | tf_op jit(solution)/shard_map/while
  103.4 8.3 %copy-start.24 = (bf16[256,256]{1,0:T(8,128)(2,1)}, bf16[256,256]{1,0:T(8,128)(2,1)S(1)}, u32[]{:S(2)}) copy-start(bf16[256,256]{1,0:T(8,128)(2,1)S(1)} %get-tuple-element.885) | copy-start | bytes 393220 | tf_op jit(solution)/shard_map/while
  104.1 2.4 copy-start.16
  114.7 0.7 copy-start.17
  117.9 0.7 copy-start.15
  118.6 0.9 copy-start.25
  118.9 0.7 copy-start.29
  119.6 19.6 %copy-start.3 = (bf16[8,128,256]{2,1,0:T(8,128)(2,1)}, bf16[8,128,256]{2,1,0:T(8,128)(2,1)S(1)}, u32[]{:S(2)}) copy-start(bf16[8,128,256]{2,1,0:T(8,128)(2,1)S(1)} %get-tuple-element.419) | copy-start | bytes 1572868
  119.6 20.3 %collective-permute-start.3 = (bf16[32,256]{1,0:T(8,128)(2,1)S(1)}, bf16[32,256]{1,0:T(8,128)(2,1)S(1)}, u32[]{:S(2)}, u32[]{:S(2)}) collective-permute-start(bf16[32,256]{1,0:T(8,128)(2,1)S(1)} %get-tuple-element.515), channel_id=1, source_target_pairs={{0,2},{2,4},{4,6},{6,8},{8,10},{10,12},{12,14},{14,16},{16,18},{18... | collective-permute-start | bytes 49160 | tf_op jit(solution)/shard_map/ppermute | solution.py:14
  134.3 84.7 %collective-permute-start.2 = (bf16[32,256]{1,0:T(8,128)(2,1)S(1)}, bf16[32,256]{1,0:T(8,128)(2,1)S(1)}, u32[]{:S(2)}, u32[]{:S(2)}) collective-permute-start(bf16[32,256]{1,0:T(8,128)(2,1)S(1)} %get-tuple-element.514), channel_id=1, source_target_pairs={{0,30},{2,0},{4,2},{6,4},{8,6},{10,8},{12,10},{14,12},{16,14},{18,... | collective-permute-start | bytes 49160 | tf_op jit(solution)/shard_map/ppermute | solution.py:14
  220.0 0.8 copy-start.14
  220.6 0.8 copy-start.12
  220.7 151.9 %all-reduce.4.cloned.1.call-start = ((), (), s32[]{:S(2)}) async-start(), calls=%async_computation.4 | async-start | bytes 3670016 | tf_op jit(solution)/shard_map/psum | solution.py:215
  222.4 42.9 %copy-start.6 = (f32[64,512]{1,0:T(8,128)S(1)}, f32[64,512]{1,0:T(8,128)}, u32[]{:S(2)}) copy-start(f32[64,512]{1,0:T(8,128)} %copy-done.5) | copy-start | bytes 393220
  222.5 0.7 copy-start.20
  223.2 0.7 copy-start.18
  372.6 2.1 copy-start.10
  374.7 1.1 copy-start.4
  375.8 1.1 copy-start.9
Sparse Core Ops, SparseCore 0:
  33.9 42.6 reduce-scatter.2
  220.8 10.2 reduce-scatter.4
  238.0 134.4 all-reduce.3
where the time goes:
time: 389 us; the launch traced here: 384 us
  waiting for transfers between devices  227 us (58%)
  blocking collectives  51.9 us (13%)
  local copies, waits for them, and re-layouts  28.9 us (7%)
  other arithmetic  24.6 us (6%)
  starting transfers between devices  23.2 us (6%)
  between operations  14.8 us (4%)
  matrix products  12.4 us (3%)
    psum x1, waiting for transfers between devices, on_device(): lax.psum((edge_wgrads[0] * edge_scale, edge_wgrads[1] * edge_scale, edge_...  106 us
    ppermute x4, waiting for transfers between devices, passed_along(): lax.ppermute(array, axis, [(i, (i + by) % count) for i in range(count)])  79.1 us
    reduce_scatter x1, waiting for transfers between devices, on_device(): lax.psum_scatter(agg_rows, 'helper', scatter_dimension=0, tiled=True)  42.2 us
    psum x1, blocking collectives, on_device(): lax.psum((edge_wgrads[0] * edge_scale, edge_wgrads[1] * edge_scale, edge_...  41.4 us
    ppermute x4, starting transfers between devices, passed_along(): lax.ppermute(array, axis, [(i, (i + by) % count) for i in range(count)])  23.1 us
    unnamed x58, local copies, waits for them, and re-layouts  11.6 us
  transfers between devices with their start and end apart: 7, of which 3 were waited for; matrix products, arithmetic and copies ran while one was open for 1% of the time, Pallas kernels for 0%

commit v1 on v0

--- a/solution.py
+++ b/solution.py
@@ -7,6 +7,7 @@
 EB = 128
 RTILE = 64
 norm_eps = 1e-05
+arrange_sectors = lambda block_in: lax.psum(lax.psum(block_in, "helper"), "band")
 
 
 def passed_along(array, axis, by):
@@ -212,7 +213,7 @@
     grad_node = node_sum + grad_out_node.astype(jnp.float32) + node_back[0][:, :features]
     edge_scale = 1.0 / math.sqrt(slot_count * edge_block * helpers * band_count)
     node_scale = 1.0 / math.sqrt(node_dev * helpers * band_count)
-    sums = lax.psum(
+    sums = arrange_sectors(
         (
             edge_wgrads[0] * edge_scale,
             edge_wgrads[1] * edge_scale,
@@ -222,8 +223,7 @@
             node_back[2] * node_scale,
             node_back[3] * node_scale,
             node_back[4] * node_scale,
-        ),
-        ("band", "helper"),
+        )
     )
     grad_edge = edge_out.reshape(slot_count * edge_block, features)
     return (

time: 389 us -> 404 us (1.039)
  waiting for transfers between devices: 227 us -> 247 us
    psum x1 -> x2, waiting for transfers between devices: 106 us -> 124 us  [the longest x1 73.4 us: lax.psum(lax.psum(block_in, 'helper'), 'band')]
    psum x1 -> x2, blocking collectives: 41.4 us -> 37.6 us  [the longest x1 32.7 us: lax.psum(lax.psum(block_in, 'helper'), 'band')]
    unnamed x58 -> x50, local copies, waits for them, and re-layouts: 11.6 us -> 10.8 us
  transfers between devices with their start and end apart: 7 -> 8, of which waited for: 3 -> 5; matrix products, arithmetic and copies ran while one was open for 1% -> 1% of each run, Pallas kernels for 0% -> 0%
where the time goes in v1:
time: 404 us; the launch traced here: 400 us
  waiting for transfers between devices  247 us (61%)
  blocking collectives  48.1 us (12%)
  local copies, waits for them, and re-layouts  28.1 us (7%)
  other arithmetic  24.7 us (6%)
  starting transfers between devices  23.3 us (6%)
  between operations  14.8 us (4%)
  matrix products  12.4 us (3%)
    ppermute x4, waiting for transfers between devices, passed_along(): lax.ppermute(array, axis, [(i, (i + by) % count) for i in range(count)])  80.9 us
    psum x1, waiting for transfers between devices, lax.psum(lax.psum(block_in, 'helper'), 'band')  73.4 us
    psum x1, waiting for transfers between devices, lax.psum(block_in, 'helper')  50.6 us
    reduce_scatter x1, waiting for transfers between devices, on_device(): lax.psum_scatter(agg_rows, 'helper', scatter_dimension=0, tiled=True)  42.2 us
    psum x1, blocking collectives, lax.psum(lax.psum(block_in, 'helper'), 'band')  32.7 us
    ppermute x4, starting transfers between devices, passed_along(): lax.ppermute(array, axis, [(i, (i + by) % count) for i in range(count)])  23.1 us
    unnamed x50, local copies, waits for them, and re-layouts  10.8 us
  transfers between devices with their start and end apart: 8, of which 5 were waited for; matrix products, arithmetic and copies ran while one was open for 1% of the time, Pallas kernels for 0%

profile of v1, /device:TPU:0, one launch (start us, length us, event | category | flops | bytes accessed | tf_op | source)
XLA Modules:
  0.0 399.6 jit_solution(13738853863955252192)
XLA Ops:
  7.3 5.9 %all_gather.6 = bf16[128,256]{1,0:T(8,128)(2,1)S(1)} all-gather(bf16[64,256]{1,0:T(8,128)(2,1)} %param.23), channel_id=1, replica_groups=mesh['band'=16,'helper'=2] {'helper'}, dimensions={0}, use_global_device_ids=true | all-gather | bytes 98304 | tf_op jit(solution)/shard_map/all_gather | solution.py:128
  14.4 4.4 %collective-permute-start.1 = (bf16[32,256]{1,0:T(8,128)(2,1)S(1)}, bf16[32,256]{1,0:T(8,128)(2,1)S(1)}, u32[]{:S(2)}, u32[]{:S(2)}) collective-permute-start(bf16[32,256]{1,0:T(8,128)(2,1)S(1)} %gather_fusion.5), channel_id=1, source_target_pairs={{0,30},{2,0},{4,2},{6,4},{8,6},{10,8},{12,10},{14,12},{16,14},{18,... | collective-permute-start | bytes 49160 | tf_op jit(solution)/shard_map/ppermute | solution.py:15
  21.5 11.5 %while.35 = (s32[]{:T(128)}, f32[128,256]{1,0:T(8,128)S(1)}, s32[]{:T(128)}, s32[8,128]{1,0:T(8,128)}, s32[8,128]{1,0:T(8,128)}, /*index=5*/bf16[192,256]{1,0:T(...) while((s32[]{:T(128)}, f32[128,256]{1,0:T(8,128)S(1)}, ...), condition=%wide.region_3.4_spmd, body=%wide.region_0.3_spmd.sunk | while | flops 72379416 | bytes 1659831 | solution.py:150
  22.3 0.9 dynamic-slice_bitcast_fusion.4
  23.2 0.8 gather_fusion
  24.8 0.8 gather_fusion.1
  25.6 1.1 fusion.120
  28.1 0.9 dynamic-slice_bitcast_fusion.4
  29.0 0.8 gather_fusion
  30.5 0.8 gather_fusion.1
  31.4 1.1 fusion.120
  34.4 42.2 %reduce-scatter.3.cloned.1.call-done = f32[64,256]{1,0:T(8,128)} async-done(((f32[128,256]{1,0:T(8,128)}), f32[64,256]{1,0:T(8,128)}) %reduce-scatter.3.cloned.1.call-update) | async-done | bytes 65552 | tf_op jit(solution)/shard_map/reduce_scatter | solution.py:151
  76.5 0.8 convert_element_type.89
  81.2 1.0 convolution_multiply_fusion.1
  82.3 0.9 convolution_multiply_fusion.2
  83.2 4.6 %all_gather.7 = bf16[128,256]{1,0:T(8,128)(2,1)S(1)} all-gather(bf16[64,256]{1,0:T(8,128)(2,1)S(1)} %slice.106), channel_id=1, replica_groups=mesh['band'=16,'helper'=2] {'helper'}, dimensions={0}, use_global_device_ids=true | all-gather | bytes 98304 | tf_op jit(solution)/shard_map/all_gather | solution.py:157
  88.0 32.5 %while.36 = (s32[]{:T(128)}, f32[192,256]{1,0:T(8,128)S(1)}, bf16[8,128,256]{2,1,0:T(8,128)(2,1)S(1)}, f32[768,256]{1,0:T(8,128)S(1)}, f32[256]{0:T(256)S(1)}, /...) while((s32[]{:T(128)}, f32[192,256]{1,0:T(8,128)S(1)}, ...), condition=%wide.region_18.19_spmd, body=%wide.region_9.18_spmd.sunk | while | flops 229600272 | bytes 8176405 | solution.py:197
  88.8 0.8 dynamic-slice_bitcast_fusion.5
  90.3 0.8 gather_fusion.2
  91.2 0.8 gather_fusion.3
  92.3 0.8 gather_fusion.4
  93.1 0.9 fusion.134
  94.3 1.0 fusion.135
  95.3 1.0 fusion.136
  97.4 1.5 scatter_custom_fusion.7
  100.8 1.5 fusion.140
  105.0 0.8 dynamic-slice_bitcast_fusion.5
  106.5 0.8 gather_fusion.2
  107.4 0.8 gather_fusion.3
  108.5 0.8 gather_fusion.4
  109.3 0.9 fusion.134
  110.5 1.0 fusion.135
  111.5 1.0 fusion.136
  113.6 1.5 scatter_custom_fusion.7
  117.0 1.5 fusion.140
  120.5 1.0 broadcast_multiply_fusion.4
  122.3 14.7 %collective-permute-start.3 = (bf16[32,256]{1,0:T(8,128)(2,1)S(1)}, bf16[32,256]{1,0:T(8,128)(2,1)S(1)}, u32[]{:S(2)}, u32[]{:S(2)}) collective-permute-start(bf16[32,256]{1,0:T(8,128)(2,1)S(1)} %get-tuple-element.523), channel_id=1, source_target_pairs={{0,2},{2,4},{4,6},{6,8},{8,10},{10,12},{12,14},{14,16},{16,18},{18... | collective-permute-start | bytes 49160 | tf_op jit(solution)/shard_map/ppermute | solution.py:15
  137.0 3.9 collective-permute-start.2
  141.0 1.3 collective-permute-done.3
  142.3 79.5 %collective-permute-done.2 = bf16[32,256]{1,0:T(8,128)(2,1)S(1)} collective-permute-done((bf16[32,256]{1,0:T(8,128)(2,1)S(1)}, bf16[32,256]{1,0:T(8,128)(2,1)S(1)}, u32[]{:S(2)}, u32[]{:S(2)}) %collective-permute-start.2) | collective-permute-done | bytes 16416 | tf_op jit(solution)/shard_map/ppermute | solution.py:15
  221.9 1.0 scatter_custom_fusion.1
  223.6 50.6 %all-reduce.9.cloned.1.call-done = (f32[768,256]{1,0:T(8,128)}, f32[256,256]{1,0:T(8,128)}, f32[512,256]{1,0:T(8,128)}, f32[256,256]{1,0:T(8,128)}) async-done(((f32[768,256]{1,0:T(8,128)}, f32[256,256]{1,0:T(8,128)}, f32[512,256]{1,0:T(8,128)}, f32[256,256]{1,0:T(8,128)}), (f32[768,256]{1,0:T(8,128)}, f32[256,256]{1,0:T(8,128)}, f32[512,256]{1,0:T(8,128)}, ...) | async-done | bytes 1835024 | tf_op jit(solution)/shard_map/psum | solution.py:10
  275.6 4.9 %all-reduce.2 = (f32[256]{0:T(256)S(1)}, f32[256]{0:T(256)S(1)}, f32[256]{0:T(256)S(1)}, f32[256]{0:T(256)S(1)}) all-reduce(f32[256]{0:T(256)S(1)} %broadcast_multiply_fusion.9, f32[256]{0:T(256)S(1)} %broadcast_multiply_fusion.8, f32[256]{0:T(256)S(1)} %broadcast_multiply_fusion.7, ...), channel_id=1, replica_groups=mesh['band'=16,'helper'=2] {'helper'}, use_global_device_ids=true, to_apply=%region_23.24 | all-reduce | flops 1024 | bytes 8192 | tf_op jit(solution)/shard_map/psum | solution.py:10
  280.5 32.7 %all-reduce = (f32[256]{0:T(256)}, f32[256]{0:T(256)}, f32[256]{0:T(256)}, f32[256]{0:T(256)}) all-reduce(f32[256]{0:T(256)S(1)} %get-tuple-element.498, f32[256]{0:T(256)S(1)} %get-tuple-element.499, f32[256]{0:T(256)S(1)} %get-tuple-element.500, f32[256]{0:T(256)S(1)} %get-tuple-element.501), channel_id=1, replica_groups=mesh['band'=16,'helper'=2] {'band'}, use_global_device_ids=true, to_apply=%region_24.25 | all-reduce | flops 1024 | bytes 8192 | tf_op jit(solution)/shard_map/psum | solution.py:10
  313.2 1.4 fusion.47
  314.6 73.4 %all-reduce.7.cloned.1.call-done = (f32[768,256]{1,0:T(8,128)}, f32[256,256]{1,0:T(8,128)}, f32[512,256]{1,0:T(8,128)}, f32[256,256]{1,0:T(8,128)}) async-done(((f32[768,256]{1,0:T(8,128)}, f32[256,256]{1,0:T(8,128)}, f32[512,256]{1,0:T(8,128)}, f32[256,256]{1,0:T(8,128)}), (f32[768,256]{1,0:T(8,128)}, f32[256,256]{1,0:T(8,128)}, f32[512,256]{1,0:T(8,128)}, ...) | async-done | bytes 1835024 | tf_op jit(solution)/shard_map/psum | solution.py:10
  388.0 2.1 copy.69
  391.2 0.8 copy.71
  (175 shorter events, 30.4 us)
Async XLA Ops:
  7.2 70.2 %copy-start = (bf16[512,256]{1,0:T(8,128)(2,1)S(1)}, bf16[512,256]{1,0:T(8,128)(2,1)}, u32[]{:S(2)}) copy-start(bf16[512,256]{1,0:T(8,128)(2,1)} %param.36) | copy-start | bytes 786436
  7.2 6.0 %copy-start.26 = (s32[1,32]{1,0:T(1,128)S(1)}, s32[1,32]{1,0:T(1,128)}, u32[]{:S(2)}) copy-start(s32[1,32]{1,0:T(1,128)} %param.30) | copy-start | bytes 388
  7.2 13.6 %copy-start.1 = (bf16[768,256]{1,0:T(8,128)(2,1)S(1)}, bf16[768,256]{1,0:T(8,128)(2,1)}, u32[]{:S(2)}) copy-start(bf16[768,256]{1,0:T(8,128)(2,1)} %param.32) | copy-start | bytes 1179652
  7.2 69.3 %reduce-scatter.3.cloned.1.call-start = ((), (), s32[]{:S(2)}) async-start(), calls=%async_computation.2 | async-start | bytes 196608 | tf_op jit(solution)/shard_map/reduce_scatter | solution.py:151
  13.2 0.5 copy-start.17
  14.3 6.4 %collective-permute-start = (bf16[32,256]{1,0:T(8,128)(2,1)S(1)}, bf16[32,256]{1,0:T(8,128)(2,1)S(1)}, u32[]{:S(2)}, u32[]{:S(2)}) collective-permute-start(bf16[32,256]{1,0:T(8,128)(2,1)S(1)} %gather_fusion.5), channel_id=1, source_target_pairs={{0,2},{2,4},{4,6},{6,8},{8,10},{10,12},{12,14},{14,16},{16,18},{18... | collective-permute-start | bytes 49160 | tf_op jit(solution)/shard_map/ppermute | solution.py:15
  14.4 6.4 %collective-permute-start.1 = (bf16[32,256]{1,0:T(8,128)(2,1)S(1)}, bf16[32,256]{1,0:T(8,128)(2,1)S(1)}, u32[]{:S(2)}, u32[]{:S(2)}) collective-permute-start(bf16[32,256]{1,0:T(8,128)(2,1)S(1)} %gather_fusion.5), channel_id=1, source_target_pairs={{0,30},{2,0},{4,2},{6,4},{8,6},{10,8},{12,10},{14,12},{16,14},{18,... | collective-permute-start | bytes 49160 | tf_op jit(solution)/shard_map/ppermute | solution.py:15
  18.8 0.7 copy-start.27
  18.8 2.0 copy-start.19
  20.8 0.7 copy-start.23
  33.0 0.7 copy-start.2
  33.7 0.7 copy-start.28
  33.7 240.5 %all-reduce.9.cloned.1.call-start = ((), (), s32[]{:S(2)}) async-start(), calls=%async_computation.5 | async-start | bytes 3670016 | tf_op jit(solution)/shard_map/psum | solution.py:10
  34.4 43.0 %copy-start.7 = (bf16[64,256]{1,0:T(8,128)(2,1)S(1)}, bf16[64,256]{1,0:T(8,128)(2,1)}, u32[]{:S(2)}) copy-start(bf16[64,256]{1,0:T(8,128)(2,1)} %param.23) | copy-start | bytes 98308
  34.4 43.0 %copy-start.15 = (f32[256]{0:T(256)S(1)}, f32[256]{0:T(256)}, u32[]{:S(2)}) copy-start(f32[256]{0:T(256)} %param.37) | copy-start | bytes 3076
  77.4 0.9 copy-start.18
  77.4 0.9 copy-start.22
  78.6 0.8 copy-start.8
  81.2 2.0 copy-start.5
  88.0 4.0 %copy-start.24 = (f32[256]{0:T(256)}, f32[256]{0:T(256)S(1)}, u32[]{:S(2)}) copy-start(f32[256]{0:T(256)S(1)} %get-tuple-element.892) | copy-start | bytes 3076 | tf_op jit(solution)/shard_map/while
  88.0 8.3 %copy-start.20 = (bf16[256,256]{1,0:T(8,128)(2,1)}, bf16[256,256]{1,0:T(8,128)(2,1)S(1)}, u32[]{:S(2)}) copy-start(bf16[256,256]{1,0:T(8,128)(2,1)S(1)} %get-tuple-element.893) | copy-start | bytes 393220 | tf_op jit(solution)/shard_map/while
  88.8 2.4 copy-start.12
  99.4 0.7 copy-start.13
  102.6 0.7 copy-start.11
  103.3 0.9 copy-start.21
  103.6 0.7 copy-start.25
  104.3 4.0 copy-start.24
  104.3 8.3 %copy-start.20 = (bf16[256,256]{1,0:T(8,128)(2,1)}, bf16[256,256]{1,0:T(8,128)(2,1)S(1)}, u32[]{:S(2)}) copy-start(bf16[256,256]{1,0:T(8,128)(2,1)S(1)} %get-tuple-element.893) | copy-start | bytes 393220 | tf_op jit(solution)/shard_map/while
  105.0 2.4 copy-start.12
  115.6 0.7 copy-start.13
  118.8 0.7 copy-start.11
  119.5 0.9 copy-start.21
  119.8 0.7 copy-start.25
  120.5 1.1 copy-start.3
  122.3 190.9 %reduce-scatter.5.cloned.1.call-start = ((), (), s32[]{:S(2)}) async-start(), calls=%async_computation.3 | async-start | bytes 98304 | tf_op jit(solution)/shard_map/reduce_scatter | solution.py:210
  122.3 20.0 %collective-permute-start.3 = (bf16[32,256]{1,0:T(8,128)(2,1)S(1)}, bf16[32,256]{1,0:T(8,128)(2,1)S(1)}, u32[]{:S(2)}, u32[]{:S(2)}) collective-permute-start(bf16[32,256]{1,0:T(8,128)(2,1)S(1)} %get-tuple-element.523), channel_id=1, source_target_pairs={{0,2},{2,4},{4,6},{6,8},{8,10},{10,12},{12,14},{14,16},{16,18},{18... | collective-permute-start | bytes 49160 | tf_op jit(solution)/shard_map/ppermute | solution.py:15
  137.0 84.8 %collective-permute-start.2 = (bf16[32,256]{1,0:T(8,128)(2,1)S(1)}, bf16[32,256]{1,0:T(8,128)(2,1)S(1)}, u32[]{:S(2)}, u32[]{:S(2)}) collective-permute-start(bf16[32,256]{1,0:T(8,128)(2,1)S(1)} %get-tuple-element.522), channel_id=1, source_target_pairs={{0,30},{2,0},{4,2},{6,4},{8,6},{10,8},{12,10},{14,12},{16,14},{18,... | collective-permute-start | bytes 49160 | tf_op jit(solution)/shard_map/ppermute | solution.py:15
  223.5 164.5 %all-reduce.7.cloned.1.call-start = ((), (), s32[]{:S(2)}) async-start(), calls=%async_computation.4 | async-start | bytes 3670016 | tf_op jit(solution)/shard_map/psum | solution.py:10
  274.2 39.0 %copy-start.6 = (f32[64,512]{1,0:T(8,128)S(1)}, f32[64,512]{1,0:T(8,128)}, u32[]{:S(2)}) copy-start(f32[64,512]{1,0:T(8,128)} %copy-done.5) | copy-start | bytes 393220
  274.2 0.7 copy-start.16
  274.9 0.7 copy-start.14
  388.0 2.1 copy-start.10
  390.1 1.1 copy-start.4
  391.2 1.1 copy-start.9
Sparse Core Ops, SparseCore 0:
  33.8 42.6 reduce-scatter.2
  122.4 151.7 all-reduce.8
  276.9 10.0 reduce-scatter.4
  290.7 97.2 all-reduce.6
